TPU v7x, 512 devices: a whole 4x8x8 slice. The times are simulated.
512 devices in a mesh: gx: 32 (over z, y_lo), gy: 16 (over x, y_hi, core).
Axes of the slice: x: 4, y: 8 (y_hi: 2, y_lo: 4; y = y_hi * 4 + y_lo), z: 8, core: 2. Of those that a mesh axis runs over, the one named last changes fastest.
Arguments:
- ensemble: float32 [40, 8, 64, 4096], P(None, None, 'gy', 'gx'), may hold values from 0.2 to 2
- courant_x: float32 [2, 64, 4096], P(None, 'gy', 'gx'), may hold values from -0.4 to 0.4
- courant_y: float32 [2, 64, 4096], P(None, 'gy', 'gx'), may hold values from -0.4 to 0.4
- diffusion: float32 [64, 4096], P('gy', 'gx'), may hold values from 0.02 to 0.12
- mixing: float32 [64, 4096], P('gy', 'gx'), may hold values from 0.02 to 0.2
- growth: float32 [2, 64, 4096], P(None, 'gy', 'gx'), may hold values from 0.05 to 0.5
- land_sea: int32 [64, 4096], P('gy', 'gx'), may hold values 0 or 1
- obs_cell: int32 [2, 1024], replicated, may hold values from 0 to 262143, as said below
- obs_value: float32 [2, 1024], replicated, may hold values from 0.2 to 2
- observation_variance: float32 [2, 1024], replicated, may hold values from 0.05 to 0.5
- obs_perturb: float32 [2, 1024, 40], replicated, may hold values from -4 to 4
- radius: int32 [1], replicated, may hold values from 32 to 64
Outputs:
- analysis: float32 [40, 8, 64, 4096], P(None, None, 'gy', 'gx')
Inputs may be any that keep to these rules, and one draw needn't show every extreme that they name: obs_cell[b, k] is row * 4096 + column of the observed cell; with tiles of 4 rows and 128 columns, in each batch no tile holds more than 8 observed cells and some tile holds exactly 8.
All inputs are finite; a program needn't handle non-finite values. No bound on the sum of `land_sea` on one device may be relied on, other than what follows from the above.
Results may differ from a plain program's by a relative error of at most 0.0003.
Values sent between devices are 32-bit elements; how exact they have to be, the bound alone decides.
A program may use at most 64 MiB of HBM per device.

v0:
```python
import jax
import jax.numpy as jnp
from jax import lax
from jax.sharding import PartitionSpec as P

CAP = 8


def padded_2(x, sides, width):
    for axis, dim in sides:
        size, length = (lax.axis_size(axis), x.shape[dim])
        up = [(i, (i + 1) % size) for i in range(size)]
        down = [(j, i) for i, j in up]
        last = lax.slice_in_dim(x, length - width, length, axis=dim)
        initial = lax.slice_in_dim(x, 0, width, axis=dim)
        before = lax.ppermute(last, axis, up)
        after = lax.ppermute(initial, axis, down)
        x = jnp.concatenate([before, x, after], axis=dim)
    return x


def upwind(minus_two, minus_one, center, plus_one, plus_two, courant):
    rising = (2.0 * plus_one + 3.0 * center - 6.0 * minus_one + minus_two) / 6.0
    falling = (-plus_two + 6.0 * plus_one - 3.0 * center - 2.0 * minus_one) / 6.0
    return -(jnp.maximum(courant, 0.0) * rising + jnp.minimum(courant, 0.0) * falling)


def transport(padded, courant_x, courant_y, diffusion):
    row_count = padded.shape[-2] - 4
    columns = padded.shape[-1] - 4

    def offset(row_shift, col_shift):
        return padded[
            ..., 2 + row_shift : 2 + row_shift + row_count, 2 + col_shift : 2 + col_shift + columns
        ]

    center = offset(0, 0)
    along_x = upwind(
        offset(0, -2), offset(0, -1), center, offset(0, 1), offset(0, 2), courant_x[:, None]
    )
    along_y = upwind(
        offset(-2, 0), offset(-1, 0), center, offset(1, 0), offset(2, 0), courant_y[:, None]
    )
    spread = offset(0, 1) + offset(0, -1) + offset(1, 0) + offset(-1, 0) - 4.0 * center
    return (center, along_x + along_y + diffusion * spread)


def tendency(fields, growth, mixing):
    nutrient = fields[..., 0, :, :]
    plankton = fields[..., 1, :, :]
    grazer = fields[..., 2, :, :]
    detritus = fields[..., 3, :, :]
    uptake = growth * jnp.abs(nutrient) / (jnp.abs(nutrient) + 0.5) * plankton
    grazing = 0.3 * grazer * jnp.abs(plankton) / (jnp.abs(plankton) + 0.5)
    biology = jnp.stack(
        [
            -uptake + 0.1 * detritus,
            uptake - grazing - 0.05 * plankton,
            0.3 * grazing - 0.05 * grazer,
            0.7 * grazing + 0.05 * plankton + 0.05 * grazer - 0.1 * detritus,
        ],
        axis=-3,
    )
    upper_level = fields[..., 0, :, :, :]
    lower_level = fields[..., 1, :, :, :]
    vertical = jnp.stack(
        [mixing * (lower_level - upper_level), mixing * (upper_level - lower_level)], axis=-4
    )
    return biology + vertical


def build_slots(
    present_state,
    cells,
    values,
    variances,
    perturbs,
    tile_id,
    tiles_y,
    row_start,
    col_start,
    total_cols,
):
    members = present_state.shape[0]
    tile_rows = present_state.shape[2]
    tile_cols = present_state.shape[3]
    obs_rows = cells // total_cols
    obs_cols = cells % total_cols
    owners = obs_cols // tile_cols * tiles_y + obs_rows // tile_rows
    ownership_mask = owners == tile_id
    slot_rank = jnp.cumsum(ownership_mask.astype(jnp.int32)) - 1
    slot_hot = (slot_rank[None, :] == jnp.arange(CAP, dtype=jnp.int32)[:, None]) & ownership_mask[
        None, :
    ]
    slot_float = slot_hot.astype(jnp.float32)
    local_cell = (obs_rows - row_start) * tile_cols + (obs_cols - col_start)
    slot_cell = jnp.sum(jnp.where(slot_hot, local_cell[None, :], 0), axis=1)
    filled = jnp.sum(slot_float, axis=1)
    cell_hot = (
        (slot_cell[:, None] == jnp.arange(tile_rows * tile_cols, dtype=jnp.int32)[None, :])
        & (filled[:, None] > 0.0)
    ).astype(jnp.float32)
    plankton_field = present_state[:, 1].reshape(members, tile_rows * tile_cols)
    prior_slots = lax.dot_general(
        cell_hot, plankton_field, (((1,), (1,)), ((), ())), precision=lax.Precision.HIGHEST
    )
    slot_value = jnp.dot(slot_float, values, precision=lax.Precision.HIGHEST)
    slot_var = jnp.dot(slot_float, variances, precision=lax.Precision.HIGHEST)
    slot_noise = jnp.dot(slot_float, perturbs, precision=lax.Precision.HIGHEST)
    slot_row = jnp.dot(slot_float, obs_rows.astype(jnp.float32), precision=lax.Precision.HIGHEST)
    slot_col = jnp.dot(slot_float, obs_cols.astype(jnp.float32), precision=lax.Precision.HIGHEST)
    anomaly = prior_slots - jnp.mean(prior_slots, axis=1, keepdims=True)
    spread_var = jnp.sum(anomaly * anomaly, axis=1) / (members - 1)
    obs_scale = filled / ((members - 1) * (spread_var + slot_var + (1.0 - filled)))
    innovation = slot_value[:, None] + jnp.sqrt(slot_var)[:, None] * slot_noise - prior_slots
    record = jnp.concatenate(
        [anomaly, innovation, obs_scale[:, None], slot_row[:, None], slot_col[:, None]], axis=1
    )
    return record[None]


def local(
    ensemble,
    courant_x,
    courant_y,
    diffusion,
    mixing,
    growth,
    land_sea,
    obs_cell,
    obs_value,
    observation_variance,
    obs_perturb,
    radius,
):
    members, fields, tile_rows, tile_cols = ensemble.shape
    levels = courant_x.shape[0]
    tiles_x = lax.axis_size("gx")
    tiles_y = lax.axis_size("gy")
    tile_x = lax.axis_index("gx")
    tile_y = lax.axis_index("gy")
    total_cols = tile_cols * tiles_x
    total_rows = tile_rows * tiles_y
    ocean_mask = land_sea.astype(jnp.float32)
    padded = padded_2(ensemble, (("gx", 3), ("gy", 2)), 2)
    global_row = tile_y * tile_rows + jnp.arange(tile_rows + 4, dtype=jnp.int32) - 2
    inside = (global_row >= 0) & (global_row < total_rows)
    padded = jnp.where(inside[:, None], padded, 0.0)
    padded = padded.reshape(members, levels, fields // levels, tile_rows + 4, tile_cols + 4)
    center, carried = transport(padded, courant_x, courant_y, diffusion)
    present_state = center + ocean_mask * (carried + tendency(center, growth, mixing))
    present_state = present_state.reshape(members, fields, tile_rows, tile_cols)
    tile_id = tile_x * tiles_y + tile_y
    row_start = tile_y * tile_rows
    col_start = tile_x * tile_cols
    grid_cell_count = tile_rows * tile_cols
    cell_rowf = (
        jnp.broadcast_to(
            (row_start + jnp.arange(tile_rows, dtype=jnp.int32))[:, None], (tile_rows, tile_cols)
        )
        .reshape(grid_cell_count)
        .astype(jnp.float32)
    )
    cell_colf = (
        jnp.broadcast_to(
            (col_start + jnp.arange(tile_cols, dtype=jnp.int32))[None, :], (tile_rows, tile_cols)
        )
        .reshape(grid_cell_count)
        .astype(jnp.float32)
    )
    radius_sq = radius[0].astype(jnp.float32) * radius[0].astype(jnp.float32)
    half_cols = total_cols // 2
    for batch_index in range(obs_value.shape[0]):
        record = build_slots(
            present_state,
            obs_cell[batch_index],
            obs_value[batch_index],
            observation_variance[batch_index],
            obs_perturb[batch_index],
            tile_id,
            tiles_y,
            row_start,
            col_start,
            total_cols,
        )
        column_slots = lax.all_gather(record, "gy", axis=1, tiled=True)
        nearby = padded_2(column_slots, (("gx", 0),), 1)
        member_deviation = (present_state - jnp.mean(present_state, axis=0, keepdims=True)).reshape(
            members, fields * grid_cell_count
        )
        increment = jnp.zeros((members, fields * grid_cell_count), jnp.float32)
        for column_index in range(3):
            slot_block = nearby[column_index]
            block_size = slot_block.shape[0]
            slot_anom = slot_block[:, :members]
            slot_innov = slot_block[:, members : 2 * members]
            obs_scale = slot_block[:, 2 * members]
            slot_row = slot_block[:, 2 * members + 1]
            slot_col = slot_block[:, 2 * members + 2]
            col_gap = (
                jnp.mod(slot_col[:, None] - cell_colf[None, :] + half_cols, total_cols) - half_cols
            )
            row_gap = slot_row[:, None] - cell_rowf[None, :]
            taper_weight = jnp.maximum(
                0.0, 1.0 - (row_gap * row_gap + col_gap * col_gap) / radius_sq
            )
            weight = taper_weight * obs_scale[:, None]
            covariance = lax.dot_general(
                slot_anom,
                member_deviation,
                (((1,), (0,)), ((), ())),
                precision=lax.Precision.HIGHEST,
            )
            gain_block = (
                covariance.reshape(block_size, fields, grid_cell_count) * weight[:, None, :]
            ).reshape(block_size, fields * grid_cell_count)
            increment = increment + lax.dot_general(
                slot_innov, gain_block, (((0,), (0,)), ((), ())), precision=lax.Precision.HIGHEST
            )
        present_state = present_state + ocean_mask * increment.reshape(
            members, fields, tile_rows, tile_cols
        )
    return present_state


def solution(mesh):
    placed = (
        P(None, None, "gy", "gx"),
        P(None, "gy", "gx"),
        P(None, "gy", "gx"),
        P("gy", "gx"),
        P("gy", "gx"),
        P(None, "gy", "gx"),
        P("gy", "gx"),
        P(),
        P(),
        P(),
        P(),
        P(),
    )
    return jax.shard_map(
        local, mesh=mesh, in_specs=placed, out_specs=P(None, None, "gy", "gx"), check_vma=False
    )
```

profile of v0, /device:TPU:1, one launch (start us, length us, event | category | flops | bytes accessed | tf_op | source)
XLA Modules:
  0.0 205.8 jit_solution(6187460439538034503)
XLA Ops:
  0.0 1.8 fusion.195
  1.8 0.4 copy.201
  2.2 14.5 %collective-permute-start.1 = (f32[40,8,4,2]{0,1,3,2:T(8,128)S(1)}, f32[40,8,4,2]{0,1,3,2:T(8,128)S(1)}, u32[]{:S(2)}, u32[]{:S(2)}) collective-permute-start(f32[40,8,4,2]{0,1,3,2:T(8,128)S(1)} %copy.201), channel_id=1, source_target_pairs={{16,0},{32,16},{48,32},{64,48},{80,64},{96,80},{112,96},{128,112},... | collective-permute-start | bytes 30728 | tf_op jit(solution)/shard_map/ppermute | solution.py:17
  16.8 0.4 copy.200
  17.2 1.9 collective-permute-start
  21.3 0.6 select_reduce_fusion
  21.9 0.5 broadcast_compare_fusion
  22.4 0.7 convolution_bitcast_fusion.5
  23.2 0.7 convolution_bitcast_fusion.1
  23.9 0.7 convolution_bitcast_fusion
  25.5 0.6 copy.156
  26.2 0.6 copy.154
  26.8 0.6 pad_maximum_fusion
  27.5 3.6 %collective-permute-start.3 = (f32[40,8,2,132]{3,1,2,0:T(8,128)S(1)}, f32[40,8,2,132]{3,1,2,0:T(8,128)S(1)}, u32[]{:S(2)}, u32[]{:S(2)}) collective-permute-start(f32[40,8,2,132]{3,1,2,0:T(8,128)S(1)} %get-tuple-element.42), channel_id=1, source_target_pairs={{1,0},{2,1},{3,2},{4,3},{5,4},{6,5},{7,6},{8,7},{9,8},{10,9},{11,1... | collective-permute-start | bytes 1013768 | tf_op jit(solution)/shard_map/ppermute | solution.py:17
  31.1 5.8 %collective-permute-start.2 = (f32[40,8,2,132]{3,1,2,0:T(8,128)S(1)}, f32[40,8,2,132]{3,1,2,0:T(8,128)S(1)}, u32[]{:S(2)}, u32[]{:S(2)}) collective-permute-start(f32[40,8,2,132]{3,1,2,0:T(8,128)S(1)} %get-tuple-element.41), channel_id=1, source_target_pairs={{0,1},{1,2},{2,3},{3,4},{4,5},{5,6},{6,7},{7,8},{8,9},{9,10},{10,1... | collective-permute-start | bytes 1013768 | tf_op jit(solution)/shard_map/ppermute | solution.py:16
  37.2 0.8 copy.158
  37.9 21.4 %collective-permute-done.3 = f32[40,8,2,132]{3,1,2,0:T(8,128)S(1)} collective-permute-done((f32[40,8,2,132]{3,1,2,0:T(8,128)S(1)}, f32[40,8,2,132]{3,1,2,0:T(8,128)S(1)}, u32[]{:S(2)}, u32[]{:S(2)}) %collective-permute-start.3) | collective-permute-done | bytes 337952 | tf_op jit(solution)/shard_map/ppermute | solution.py:17
  61.5 1.5 fusion.192
  64.1 27.1 %all-gather = f32[128,83]{1,0:T(8,128)S(1)} all-gather(f32[8,83]{1,0:T(8,128)S(1)} %concatenate.24), channel_id=2, replica_groups=mesh['gx'=32,'gy'=16] {'gy'}, dimensions={0}, use_global_device_ids=true | all-gather | bytes 45152 | tf_op jit(solution)/shard_map/all_gather | solution.py:186
  91.2 5.3 %collective-permute-start.4 = (f32[1,128,83]{2,1,0:T(8,128)S(1)}, f32[1,128,83]{2,1,0:T(8,128)S(1)}, u32[]{:S(2)}, u32[]{:S(2)}) collective-permute-start(f32[1,128,83]{2,1,0:T(8,128)S(1)} %bitcast.182), channel_id=1, source_target_pairs={{0,16},{16,32},{32,48},{48,64},{64,80},{80,96},{96,112},{112,128},... | collective-permute-start | bytes 127496 | tf_op jit(solution)/shard_map/ppermute | solution.py:16
  96.6 7.9 %collective-permute-start.5 = (f32[1,128,83]{2,1,0:T(8,128)S(1)}, f32[1,128,83]{2,1,0:T(8,128)S(1)}, u32[]{:S(2)}, u32[]{:S(2)}) collective-permute-start(f32[1,128,83]{2,1,0:T(8,128)S(1)} %bitcast.183), channel_id=1, source_target_pairs={{16,0},{32,16},{48,32},{64,48},{80,64},{96,80},{112,96},{128,112},... | collective-permute-start | bytes 127496 | tf_op jit(solution)/shard_map/ppermute | solution.py:17
  105.8 1.5 fusion.95
  107.3 3.1 %convolution_multiply_fusion.3 = f32[128,8,512]{2,0,1:T(8,128)} fusion(f32[128,512]{1,0:T(8,128)S(1)} %get-tuple-element.57, f32[5,8,8,512]{3,2,1,0:T(8,128)S(1)} %bitcast.166, f32[128,83]{1,0:T(8,128)S(1)} %bitcast.194), kind=kOutput, calls=%fused_computation.8 | convolution fusion | flops 252182528 | bytes 3057152 | tf_op jit(solution)/shard_map/dot_general | solution.py:208
  110.5 1.9 copy.173
  112.4 4.0 %fusion.117 = f32[40,4096]{1,0:T(8,128)} fusion(f32[128,4096]{0,1:T(8,128)S(1)} %bitcast.171, f32[128,83]{1,0:T(8,128)} %bitcast.195), kind=kOutput, calls=%fused_computation.187 | convolution fusion | flops 251658240 | bytes 2795008 | tf_op jit(solution)/shard_map/dot_general | solution.py:217
  116.4 3.1 %convolution_multiply_fusion.4 = f32[128,8,512]{2,0,1:T(8,128)} fusion(f32[128,512]{1,0:T(8,128)S(1)} %copy-done.8, f32[5,8,8,512]{3,2,1,0:T(8,128)S(1)} %bitcast.167, f32[128,83]{1,0:T(8,128)S(1)} %all-gather), kind=kOutput, calls=%fused_computation.9 | convolution fusion | flops 252182528 | bytes 3057152 | tf_op jit(solution)/shard_map/dot_general | solution.py:208
  119.6 1.9 copy.170
  121.5 3.2 %fusion.119 = f32[40,4096]{1,0:T(8,128)} fusion(f32[128,4096]{0,1:T(8,128)S(1)} %bitcast.172, f32[128,83]{1,0:T(8,128)S(1)} %all-gather), kind=kOutput, calls=%fused_computation.193 | convolution fusion | flops 251658240 | bytes 2795008 | tf_op jit(solution)/shard_map/dot_general | solution.py:217
  124.7 3.1 %convolution_multiply_fusion.5 = f32[128,8,512]{2,0,1:T(8,128)} fusion(f32[128,512]{1,0:T(8,128)S(1)} %copy-done.6, f32[5,8,8,512]{3,2,1,0:T(8,128)S(1)} %bitcast.168, f32[128,83]{1,0:T(8,128)S(1)} %bitcast.188), kind=kOutput, calls=%fused_computation.10 | convolution fusion | flops 252182528 | bytes 3057152 | tf_op jit(solution)/shard_map/dot_general | solution.py:208
  127.8 1.9 copy.167
  129.7 3.6 %fusion.1 = f32[40,4096]{1,0:T(8,128)S(1)} fusion(f32[40,4096]{1,0:T(8,128)} %fusion.117, f32[40,4096]{1,0:T(8,128)} %fusion.119, f32[128,4096]{0,1:T(8,128)S(1)} %bitcast.169, f32[128,83]{1,0:T(8,128)S(1)} %bitcast.189), kind=kOutput, calls=%fused_computation.3 | convolution fusion | flops 251985920 | bytes 4105728 | tf_op jit(solution)/shard_map/dot_general | solution.py:217
  133.4 0.4 reshape.700
  135.3 29.8 %all-gather.1 = f32[128,83]{1,0:T(8,128)S(1)} all-gather(f32[8,83]{1,0:T(8,128)S(1)} %concatenate.25), channel_id=3, replica_groups=mesh['gx'=32,'gy'=16] {'gy'}, dimensions={0}, use_global_device_ids=true | all-gather | bytes 45152 | tf_op jit(solution)/shard_map/all_gather | solution.py:186
  165.0 1.9 collective-permute-start.6
  167.0 8.2 %collective-permute-start.7 = (f32[1,128,83]{2,1,0:T(8,128)S(1)}, f32[1,128,83]{2,1,0:T(8,128)S(1)}, u32[]{:S(2)}, u32[]{:S(2)}) collective-permute-start(f32[1,128,83]{2,1,0:T(8,128)S(1)} %bitcast.181), channel_id=1, source_target_pairs={{16,0},{32,16},{48,32},{64,48},{80,64},{96,80},{112,96},{128,112},... | collective-permute-start | bytes 127496 | tf_op jit(solution)/shard_map/ppermute | solution.py:17
  175.2 0.4 reshape.702
  176.9 1.5 fusion.86
  178.4 3.1 %convolution_multiply_fusion = f32[128,8,512]{2,0,1:T(8,128)} fusion(f32[128,512]{1,0:T(8,128)S(1)} %get-tuple-element.52, f32[5,8,8,512]{3,2,1,0:T(8,128)S(1)} %bitcast.163, f32[128,83]{1,0:T(8,128)S(1)} %bitcast.191), kind=kOutput, calls=%fused_computation.5 | convolution fusion | flops 252182528 | bytes 3057152 | tf_op jit(solution)/shard_map/dot_general | solution.py:208
  181.5 1.9 copy.187
  183.4 4.0 %fusion.112 = f32[40,4096]{1,0:T(8,128)} fusion(f32[128,4096]{0,1:T(8,128)S(1)} %bitcast.173, f32[128,83]{1,0:T(8,128)} %bitcast.192), kind=kOutput, calls=%fused_computation.170 | convolution fusion | flops 251658240 | bytes 2795008 | tf_op jit(solution)/shard_map/dot_general | solution.py:217
  187.5 3.1 %convolution_multiply_fusion.1 = f32[128,8,512]{2,0,1:T(8,128)} fusion(f32[128,512]{1,0:T(8,128)S(1)} %copy-done.7, f32[5,8,8,512]{3,2,1,0:T(8,128)S(1)} %bitcast.164, f32[128,83]{1,0:T(8,128)S(1)} %all-gather.1), kind=kOutput, calls=%fused_computation.6 | convolution fusion | flops 252182528 | bytes 3057152 | tf_op jit(solution)/shard_map/dot_general | solution.py:208
  190.6 1.9 copy.184
  192.5 3.2 %fusion.114 = f32[40,4096]{1,0:T(8,128)} fusion(f32[128,4096]{0,1:T(8,128)S(1)} %bitcast.174, f32[128,83]{1,0:T(8,128)S(1)} %all-gather.1), kind=kOutput, calls=%fused_computation.176 | convolution fusion | flops 251658240 | bytes 2795008 | tf_op jit(solution)/shard_map/dot_general | solution.py:217
  195.7 3.1 %convolution_multiply_fusion.2 = f32[128,8,512]{2,0,1:T(8,128)} fusion(f32[128,512]{1,0:T(8,128)S(1)} %copy-done.5, f32[5,8,8,512]{3,2,1,0:T(8,128)S(1)} %bitcast.165, f32[128,83]{1,0:T(8,128)S(1)} %bitcast.185), kind=kOutput, calls=%fused_computation.7 | convolution fusion | flops 252182528 | bytes 3057152 | tf_op jit(solution)/shard_map/dot_general | solution.py:208
  198.8 1.9 copy.181
  200.7 3.6 %fusion = f32[40,4096]{1,0:T(8,128)S(1)} fusion(f32[40,4096]{1,0:T(8,128)} %fusion.112, f32[40,4096]{1,0:T(8,128)} %fusion.114, f32[128,4096]{0,1:T(8,128)S(1)} %bitcast.170, f32[128,83]{1,0:T(8,128)S(1)} %bitcast.186), kind=kOutput, calls=%fused_computation.1 | convolution fusion | flops 251985920 | bytes 4105728 | tf_op jit(solution)/shard_map/dot_general | solution.py:217
  204.3 0.4 reshape.706
  204.8 1.0 multiply_add_fusion.2
  (137 shorter events, 9.5 us)
Async XLA Ops:
  0.0 24.8 %copy-start = (f32[40,8,4,128]{3,2,1,0:T(4,128)S(1)}, f32[40,8,4,128]{3,2,1,0:T(4,128)}, u32[]{:S(2)}) copy-start(f32[40,8,4,128]{3,2,1,0:T(4,128)} %param.12) | copy-start | bytes 1966084
  0.0 19.1 %copy-start.11 = (s32[2,1024]{1,0:T(2,128)S(1)}, s32[2,1024]{1,0:T(2,128)}, u32[]{:S(2)}) copy-start(s32[2,1024]{1,0:T(2,128)} %param.19) | copy-start | bytes 24580
  0.0 22.4 %copy-start.26 = (f32[2,1024]{1,0:T(2,128)S(1)}, f32[2,1024]{1,0:T(2,128)}, u32[]{:S(2)}) copy-start(f32[2,1024]{1,0:T(2,128)} %param.20) | copy-start | bytes 24580
  1.8 23.0 %copy-start.21 = (s32[4,128]{1,0:T(4,128)S(1)}, s32[4,128]{1,0:T(4,128)}, u32[]{:S(2)}) copy-start(s32[4,128]{1,0:T(4,128)} %param.18) | copy-start | bytes 6148
  2.2 23.3 %collective-permute-start.1 = (f32[40,8,4,2]{0,1,3,2:T(8,128)S(1)}, f32[40,8,4,2]{0,1,3,2:T(8,128)S(1)}, u32[]{:S(2)}, u32[]{:S(2)}) collective-permute-start(f32[40,8,4,2]{0,1,3,2:T(8,128)S(1)} %copy.201), channel_id=1, source_target_pairs={{16,0},{32,16},{48,32},{64,48},{80,64},{96,80},{112,96},{128,112},... | collective-permute-start | bytes 30728 | tf_op jit(solution)/shard_map/ppermute | solution.py:17
  17.2 8.9 %collective-permute-start = (f32[40,8,4,2]{0,1,3,2:T(8,128)S(1)}, f32[40,8,4,2]{0,1,3,2:T(8,128)S(1)}, u32[]{:S(2)}, u32[]{:S(2)}) collective-permute-start(f32[40,8,4,2]{0,1,3,2:T(8,128)S(1)} %copy.200), channel_id=1, source_target_pairs={{0,16},{16,32},{32,48},{48,64},{64,80},{80,96},{96,112},{112,128},... | collective-permute-start | bytes 30728 | tf_op jit(solution)/shard_map/ppermute | solution.py:16
  19.3 6.8 %copy-start.12 = (pred[1024]{0:T(1024)(128)(4,1)}, pred[1024]{0:T(1024)(128)(4,1)S(1)}, u32[]{:S(2)}) copy-start(pred[1024]{0:T(1024)(128)(4,1)S(1)} %get-tuple-element.25) | copy-start | bytes 3076
  21.3 1.9 copy-start.24
  27.4 9.7 %copy-start.15 = (f32[2,4,128]{2,1,0:T(4,128)S(1)}, f32[2,4,128]{2,1,0:T(4,128)}, u32[]{:S(2)}) copy-start(f32[2,4,128]{2,1,0:T(4,128)} %param.14) | copy-start | bytes 12292
  27.4 9.7 %copy-start.16 = (f32[2,4,128]{2,1,0:T(4,128)S(1)}, f32[2,4,128]{2,1,0:T(4,128)}, u32[]{:S(2)}) copy-start(f32[2,4,128]{2,1,0:T(4,128)} %param.13) | copy-start | bytes 12292
  27.5 31.9 %collective-permute-start.3 = (f32[40,8,2,132]{3,1,2,0:T(8,128)S(1)}, f32[40,8,2,132]{3,1,2,0:T(8,128)S(1)}, u32[]{:S(2)}, u32[]{:S(2)}) collective-permute-start(f32[40,8,2,132]{3,1,2,0:T(8,128)S(1)} %get-tuple-element.42), channel_id=1, source_target_pairs={{1,0},{2,1},{3,2},{4,3},{5,4},{6,5},{7,6},{8,7},{9,8},{10,9},{11,1... | collective-permute-start | bytes 1013768 | tf_op jit(solution)/shard_map/ppermute | solution.py:17
  31.1 28.6 %collective-permute-start.2 = (f32[40,8,2,132]{3,1,2,0:T(8,128)S(1)}, f32[40,8,2,132]{3,1,2,0:T(8,128)S(1)}, u32[]{:S(2)}, u32[]{:S(2)}) collective-permute-start(f32[40,8,2,132]{3,1,2,0:T(8,128)S(1)} %get-tuple-element.41), channel_id=1, source_target_pairs={{0,1},{1,2},{2,3},{3,4},{4,5},{5,6},{6,7},{7,8},{8,9},{9,10},{10,1... | collective-permute-start | bytes 1013768 | tf_op jit(solution)/shard_map/ppermute | solution.py:16
  60.2 0.7 copy-start.19
  60.2 0.9 copy-start.14
  60.8 0.7 copy-start.20
  61.5 2.0 copy-start.27
  61.5 2.3 %copy-start.9 = (f32[2,1024,40]{1,2,0:T(8,128)S(1)}, f32[2,1024,40]{1,2,0:T(8,128)}, u32[]{:S(2)}) copy-start(f32[2,1024,40]{1,2,0:T(8,128)} %param.22) | copy-start | bytes 983044
  91.2 14.0 %collective-permute-start.4 = (f32[1,128,83]{2,1,0:T(8,128)S(1)}, f32[1,128,83]{2,1,0:T(8,128)S(1)}, u32[]{:S(2)}, u32[]{:S(2)}) collective-permute-start(f32[1,128,83]{2,1,0:T(8,128)S(1)} %bitcast.182), channel_id=1, source_target_pairs={{0,16},{16,32},{32,48},{48,64},{64,80},{80,96},{96,112},{112,128},... | collective-permute-start | bytes 127496 | tf_op jit(solution)/shard_map/ppermute | solution.py:16
  96.6 9.0 %collective-permute-start.5 = (f32[1,128,83]{2,1,0:T(8,128)S(1)}, f32[1,128,83]{2,1,0:T(8,128)S(1)}, u32[]{:S(2)}, u32[]{:S(2)}) collective-permute-start(f32[1,128,83]{2,1,0:T(8,128)S(1)} %bitcast.183), channel_id=1, source_target_pairs={{16,0},{32,16},{48,32},{64,48},{80,64},{96,80},{112,96},{128,112},... | collective-permute-start | bytes 127496 | tf_op jit(solution)/shard_map/ppermute | solution.py:17
  104.9 2.4 %copy-start.1 = (f32[40,4096]{1,0:T(8,128)}, f32[40,4096]{1,0:T(8,128)S(1)}, u32[]{:S(2)}) copy-start(f32[40,4096]{1,0:T(8,128)S(1)} %reshape.696) | copy-start | bytes 1966084
  105.6 1.8 copy-start.4
  112.4 4.0 %copy-start.8 = (f32[128,512]{1,0:T(8,128)S(1)}, f32[128,512]{1,0:T(8,128)}, u32[]{:S(2)}) copy-start(f32[128,512]{1,0:T(8,128)} %get-tuple-element.56) | copy-start | bytes 786436
  121.5 3.2 %copy-start.6 = (f32[128,512]{1,0:T(8,128)S(1)}, f32[128,512]{1,0:T(8,128)}, u32[]{:S(2)}) copy-start(f32[128,512]{1,0:T(8,128)} %get-tuple-element.55) | copy-start | bytes 786436
  133.3 0.8 copy-start.23
  133.3 0.8 copy-start.29
  133.3 1.3 copy-start.13
  133.3 1.3 copy-start.25
  133.4 1.3 copy-start.28
  133.4 1.6 copy-start.10
  133.4 1.6 copy-start.22
  133.4 1.7 copy-start.17
  133.4 1.8 copy-start.18
  134.1 42.0 %copy-start.2 = (f32[40,4096]{1,0:T(8,128)S(1)}, f32[40,4096]{1,0:T(8,128)}, u32[]{:S(2)}) copy-start(f32[40,4096]{1,0:T(8,128)} %copy-done.1) | copy-start | bytes 1966084
  165.0 11.3 %collective-permute-start.6 = (f32[1,128,83]{2,1,0:T(8,128)S(1)}, f32[1,128,83]{2,1,0:T(8,128)S(1)}, u32[]{:S(2)}, u32[]{:S(2)}) collective-permute-start(f32[1,128,83]{2,1,0:T(8,128)S(1)} %bitcast.180), channel_id=1, source_target_pairs={{0,16},{16,32},{32,48},{48,64},{64,80},{80,96},{96,112},{112,128},... | collective-permute-start | bytes 127496 | tf_op jit(solution)/shard_map/ppermute | solution.py:16
  167.0 9.7 %collective-permute-start.7 = (f32[1,128,83]{2,1,0:T(8,128)S(1)}, f32[1,128,83]{2,1,0:T(8,128)S(1)}, u32[]{:S(2)}, u32[]{:S(2)}) collective-permute-start(f32[1,128,83]{2,1,0:T(8,128)S(1)} %bitcast.181), channel_id=1, source_target_pairs={{16,0},{32,16},{48,32},{64,48},{80,64},{96,80},{112,96},{128,112},... | collective-permute-start | bytes 127496 | tf_op jit(solution)/shard_map/ppermute | solution.py:17
  176.6 1.8 copy-start.3
  183.4 4.0 %copy-start.7 = (f32[128,512]{1,0:T(8,128)S(1)}, f32[128,512]{1,0:T(8,128)}, u32[]{:S(2)}) copy-start(f32[128,512]{1,0:T(8,128)} %get-tuple-element.51) | copy-start | bytes 786436
  192.5 3.2 %copy-start.5 = (f32[128,512]{1,0:T(8,128)S(1)}, f32[128,512]{1,0:T(8,128)}, u32[]{:S(2)}) copy-start(f32[128,512]{1,0:T(8,128)} %get-tuple-element.50) | copy-start | bytes 786436
where the time goes:
time: 206 us
  blocking collectives  56.9 us (28%)
  starting transfers between devices  49.2 us (24%)
  matrix products  44.2 us (21%)
  local copies, waits for them, and re-layouts  21.7 us (11%)
  waiting for transfers between devices  21.6 us (10%)
  other arithmetic  10.6 us (5%)
    all_gather x2, blocking collectives, local(): column_slots = lax.all_gather(record, 'gy', axis=1, tiled=True)  56.9 us
    ppermute x4, starting transfers between devices, padded_2(): after = lax.ppermute(initial, axis, down)  34.2 us
    dot_general x6, matrix products, local(): lax.dot_general(slot_innov, gain_block, (((0,), (0,)), ((), ())), precisi...  21.6 us
    ppermute x4, waiting for transfers between devices, padded_2(): after = lax.ppermute(initial, axis, down)  21.6 us
    dot_general x6, matrix products, local(): lax.dot_general(slot_anom, member_deviation, (((1,), (0,)), ((), ())), pr...  18.8 us
    ppermute x4, starting transfers between devices, padded_2(): before = lax.ppermute(last, axis, up)  15 us
    mul x6, local copies, waits for them, and re-layouts, local(): covariance.reshape(block_size, fields, grid_cell_count) * weight[:, None, :]  11.4 us
  transfers between devices with their start and end apart: 8, of which 2 were waited for; matrix products, arithmetic and copies ran while one was open for 5% of the time, Pallas kernels for 0%

commit v1 on v0

--- a/solution.py
+++ b/solution.py
@@ -4,6 +4,13 @@
 from jax.sharding import PartitionSpec as P
 
 CAP = 8
+
+
+def gather_over(value, name, d):
+    size = lax.axis_size(name)
+    tiles = jnp.stack([value for _ in range(size)])
+    tiles = lax.all_to_all(tiles, name, split_axis=0, concat_axis=0)
+    return jnp.concatenate(tiles, axis=d)
 
 
 def padded_2(x, sides, width):
@@ -183,7 +190,7 @@
             col_start,
             total_cols,
         )
-        column_slots = lax.all_gather(record, "gy", axis=1, tiled=True)
+        column_slots = gather_over(record, "gy", 1)
         nearby = padded_2(column_slots, (("gx", 0),), 1)
         member_deviation = (present_state - jnp.mean(present_state, axis=0, keepdims=True)).reshape(
             members, fields * grid_cell_count

time: 206 us -> 181 us (0.88)
  blocking collectives: 56.9 us -> 0 us
  waiting for transfers between devices: 21.6 us -> 41.6 us
  starting transfers between devices: 49.2 us -> 59.7 us
    all_gather x2 -> x0, blocking collectives: 56.9 us -> none  [local(): column_slots = lax.all_gather(record, 'gy', axis=1, tiled=True)]
    all_to_all x0 -> x2, waiting for transfers between devices: none -> 18.6 us  [gather_over(): tiles = lax.all_to_all(tiles, name, split_axis=0, concat_axis=0)]
    all_to_all x0 -> x2, starting transfers between devices: none -> 10.2 us  [gather_over(): tiles = lax.all_to_all(tiles, name, split_axis=0, concat_axis=0)]
  transfers between devices with their start and end apart: 8 -> 10, of which waited for: 2 -> 6; matrix products, arithmetic and copies ran while one was open for 5% -> 4% of each run, Pallas kernels for 0% -> 0%
where the time goes in v1:
time: 181 us; the launch traced here: 180 us
  starting transfers between devices  59.7 us (33%)
  matrix products  43.2 us (24%)
  waiting for transfers between devices  41.6 us (23%)
  local copies, waits for them, and re-layouts  23.1 us (13%)
  other arithmetic  11.4 us (6%)
    ppermute x4, starting transfers between devices, padded_2(): after = lax.ppermute(initial, axis, down)  33.9 us
    dot_general x6, matrix products, local(): lax.dot_general(slot_innov, gain_block, (((0,), (0,)), ((), ())), precisi...  21.2 us
    ppermute x4, waiting for transfers between devices, padded_2(): after = lax.ppermute(initial, axis, down)  21.2 us
    dot_general x6, matrix products, local(): lax.dot_general(slot_anom, member_deviation, (((1,), (0,)), ((), ())), pr...  19 us
    all_to_all x2, waiting for transfers between devices, gather_over(): tiles = lax.all_to_all(tiles, name, split_axis=0, concat_axis=0)  18.6 us
    ppermute x4, starting transfers between devices, padded_2(): before = lax.ppermute(last, axis, up)  15.7 us
    mul x6, local copies, waits for them, and re-layouts, local(): covariance.reshape(block_size, fields, grid_cell_count) * weight[:, None, :]  11.4 us
    all_to_all x2, starting transfers between devices, gather_over(): tiles = lax.all_to_all(tiles, name, split_axis=0, concat_axis=0)  10.2 us
  transfers between devices with their start and end apart: 10, of which 6 were waited for; matrix products, arithmetic and copies ran while one was open for 4% of the time, Pallas kernels for 0%

profile of v1, /device:TPU:1, one launch (start us, length us, event | category | flops | bytes accessed | tf_op | source)
XLA Modules:
  0.0 180.4 jit_solution(12430591568962906472)
XLA Ops:
  0.0 1.8 fusion.195
  2.2 14.5 %collective-permute-start.1 = (f32[40,8,4,2]{0,1,3,2:T(8,128)S(1)}, f32[40,8,4,2]{0,1,3,2:T(8,128)S(1)}, u32[]{:S(2)}, u32[]{:S(2)}) collective-permute-start(f32[40,8,4,2]{0,1,3,2:T(8,128)S(1)} %copy.209), channel_id=1, source_target_pairs={{16,0},{32,16},{48,32},{64,48},{80,64},{96,80},{112,96},{128,112},... | collective-permute-start | bytes 30728 | tf_op jit(solution)/shard_map/ppermute | solution.py:24
  17.2 1.9 %collective-permute-start = (f32[40,8,4,2]{0,1,3,2:T(8,128)S(1)}, f32[40,8,4,2]{0,1,3,2:T(8,128)S(1)}, u32[]{:S(2)}, u32[]{:S(2)}) collective-permute-start(f32[40,8,4,2]{0,1,3,2:T(8,128)S(1)} %copy.208), channel_id=1, source_target_pairs={{0,16},{16,32},{32,48},{48,64},{64,80},{80,96},{96,112},{112,128},... | collective-permute-start | bytes 30728 | tf_op jit(solution)/shard_map/ppermute | solution.py:23
  21.4 0.6 broadcast_compare_fusion
  23.3 0.6 copy.176
  23.9 1.8 %collective-permute-done = f32[40,8,4,2]{0,1,3,2:T(8,128)S(1)} collective-permute-done((f32[40,8,4,2]{0,1,3,2:T(8,128)S(1)}, f32[40,8,4,2]{0,1,3,2:T(8,128)S(1)}, u32[]{:S(2)}, u32[]{:S(2)}) %collective-permute-start) | collective-permute-done | bytes 10272 | tf_op jit(solution)/shard_map/ppermute | solution.py:23
  25.8 0.6 copy.174
  27.1 4.0 %collective-permute-start.3 = (f32[40,8,2,132]{3,1,2,0:T(8,128)S(1)}, f32[40,8,2,132]{3,1,2,0:T(8,128)S(1)}, u32[]{:S(2)}, u32[]{:S(2)}) collective-permute-start(f32[40,8,2,132]{3,1,2,0:T(8,128)S(1)} %get-tuple-element.30), channel_id=1, source_target_pairs={{1,0},{2,1},{3,2},{4,3},{5,4},{6,5},{7,6},{8,7},{9,8},{10,9},{11,1... | collective-permute-start | bytes 1013768 | tf_op jit(solution)/shard_map/ppermute | solution.py:24
  31.1 5.5 %collective-permute-start.2 = (f32[40,8,2,132]{3,1,2,0:T(8,128)S(1)}, f32[40,8,2,132]{3,1,2,0:T(8,128)S(1)}, u32[]{:S(2)}, u32[]{:S(2)}) collective-permute-start(f32[40,8,2,132]{3,1,2,0:T(8,128)S(1)} %get-tuple-element.29), channel_id=1, source_target_pairs={{0,1},{1,2},{2,3},{3,4},{4,5},{5,6},{6,7},{7,8},{8,9},{9,10},{10,1... | collective-permute-start | bytes 1013768 | tf_op jit(solution)/shard_map/ppermute | solution.py:23
  36.8 0.8 copy.178
  37.5 19.6 %collective-permute-done.3 = f32[40,8,2,132]{3,1,2,0:T(8,128)S(1)} collective-permute-done((f32[40,8,2,132]{3,1,2,0:T(8,128)S(1)}, f32[40,8,2,132]{3,1,2,0:T(8,128)S(1)}, u32[]{:S(2)}, u32[]{:S(2)}) %collective-permute-start.3) | collective-permute-done | bytes 337952 | tf_op jit(solution)/shard_map/ppermute | solution.py:24
  59.3 1.5 fusion.192
  62.1 0.7 stack.20
  62.8 5.1 %all-to-all-start = ((f32[16,1,8,83]{3,2,1,0:T(8,128)}), f32[16,1,8,83]{3,2,1,0:T(8,128)S(1)}, u32[]{:S(2)}, u32[]{:S(2)}) async-start(f32[16,1,8,83]{3,2,1,0:T(8,128)} %stack.20), calls=%async_computation | async-start | bytes 131072 | tf_op jit(solution)/shard_map/all_to_all | solution.py:12
  68.2 9.4 %all-to-all-done = f32[16,1,8,83]{3,2,1,0:T(8,128)S(1)} async-done(((f32[16,1,8,83]{3,2,1,0:T(8,128)}), f32[16,1,8,83]{3,2,1,0:T(8,128)S(1)}, u32[]{:S(2)}, u32[]{:S(2)}) %all-to-all-start) | async-done | bytes 42528 | tf_op jit(solution)/shard_map/all_to_all | solution.py:12
  77.7 6.4 %collective-permute-start.4 = (f32[1,128,83]{1,2,0:T(8,128)S(1)}, f32[1,128,83]{1,2,0:T(8,128)S(1)}, u32[]{:S(2)}, u32[]{:S(2)}) collective-permute-start(f32[1,128,83]{1,2,0:T(8,128)S(1)} %copy.184), channel_id=1, source_target_pairs={{0,16},{16,32},{32,48},{48,64},{64,80},{80,96},{96,112},{112,128},... | collective-permute-start | bytes 127496 | tf_op jit(solution)/shard_map/ppermute | solution.py:23
  84.1 7.2 %collective-permute-start.5 = (f32[1,128,83]{1,2,0:T(8,128)S(1)}, f32[1,128,83]{1,2,0:T(8,128)S(1)}, u32[]{:S(2)}, u32[]{:S(2)}) collective-permute-start(f32[1,128,83]{1,2,0:T(8,128)S(1)} %copy.184), channel_id=1, source_target_pairs={{16,0},{32,16},{48,32},{64,48},{80,64},{96,80},{112,96},{128,112},... | collective-permute-start | bytes 127496 | tf_op jit(solution)/shard_map/ppermute | solution.py:24
  91.6 0.9 collective-permute-done.5
  92.4 1.5 fusion.95
  94.0 3.2 %convolution_multiply_fusion.3 = f32[128,8,512]{2,0,1:T(8,128)} fusion(f32[128,512]{1,0:T(8,128)S(1)} %get-tuple-element.57, f32[5,8,8,512]{3,2,1,0:T(8,128)S(1)} %bitcast.194, f32[128,83]{0,1:T(8,128)S(1)} %bitcast.231), kind=kOutput, calls=%fused_computation.8 | convolution fusion | flops 252182528 | bytes 3035136 | tf_op jit(solution)/shard_map/dot_general | solution.py:215
  97.2 1.9 %copy.193 = f32[128,8,512]{0,2,1:T(8,128)S(1)} copy(f32[128,8,512]{2,0,1:T(8,128)} %convolution_multiply_fusion.3) | data formatting | bytes 4194304 | tf_op jit(solution)/shard_map/mul | solution.py:222
  99.1 3.9 %fusion.131 = f32[40,4096]{1,0:T(8,128)} fusion(f32[128,4096]{0,1:T(8,128)S(1)} %bitcast.199, f32[128,83]{0,1:T(8,128)} %bitcast.232), kind=kOutput, calls=%fused_computation.192 | convolution fusion | flops 251658240 | bytes 2772992 | tf_op jit(solution)/shard_map/dot_general | solution.py:224
  103.0 3.1 %convolution_multiply_fusion.4 = f32[128,8,512]{2,0,1:T(8,128)} fusion(f32[128,512]{1,0:T(8,128)S(1)} %copy-done.6, f32[5,8,8,512]{3,2,1,0:T(8,128)S(1)} %bitcast.195, f32[128,83]{1,0:T(8,128)S(1)} %bitcast.210), kind=kOutput, calls=%fused_computation.9 | convolution fusion | flops 252182528 | bytes 3057152 | tf_op jit(solution)/shard_map/dot_general | solution.py:215
  106.1 1.9 %copy.190 = f32[128,8,512]{0,2,1:T(8,128)S(1)} copy(f32[128,8,512]{2,0,1:T(8,128)} %convolution_multiply_fusion.4) | data formatting | bytes 4194304 | tf_op jit(solution)/shard_map/mul | solution.py:222
  108.0 3.2 %fusion.114 = f32[40,4096]{1,0:T(8,128)} fusion(f32[128,4096]{0,1:T(8,128)S(1)} %bitcast.200, f32[128,83]{1,0:T(8,128)S(1)} %bitcast.211), kind=kOutput, calls=%fused_computation.176 | convolution fusion | flops 251658240 | bytes 2795008 | tf_op jit(solution)/shard_map/dot_general | solution.py:224
  111.2 3.2 %convolution_multiply_fusion.5 = f32[128,8,512]{2,0,1:T(8,128)} fusion(f32[128,512]{1,0:T(8,128)S(1)} %copy-done.4, f32[5,8,8,512]{3,2,1,0:T(8,128)S(1)} %bitcast.196, f32[128,83]{0,1:T(8,128)S(1)} %bitcast.225), kind=kOutput, calls=%fused_computation.10 | convolution fusion | flops 252182528 | bytes 3035136 | tf_op jit(solution)/shard_map/dot_general | solution.py:215
  114.4 1.9 %copy.187 = f32[128,8,512]{0,2,1:T(8,128)S(1)} copy(f32[128,8,512]{2,0,1:T(8,128)} %convolution_multiply_fusion.5) | data formatting | bytes 4194304 | tf_op jit(solution)/shard_map/mul | solution.py:222
  116.3 3.6 %fusion.1 = f32[40,4096]{1,0:T(8,128)S(1)} fusion(f32[40,4096]{1,0:T(8,128)} %fusion.131, f32[40,4096]{1,0:T(8,128)} %fusion.114, f32[128,4096]{0,1:T(8,128)S(1)} %bitcast.197, f32[128,83]{0,1:T(8,128)S(1)} %bitcast.226), kind=kOutput, calls=%fused_computation.3 | convolution fusion | flops 251985920 | bytes 4083712 | tf_op jit(solution)/shard_map/dot_general | solution.py:224
  119.9 1.3 reshape.711
  121.6 1.4 copy_add_fusion
  123.8 1.1 fusion.3
  125.0 0.6 stack.21
  125.7 5.1 %all-to-all-start.1 = ((f32[16,1,8,83]{3,2,1,0:T(8,128)}), f32[16,1,8,83]{3,2,1,0:T(8,128)S(1)}, u32[]{:S(2)}, u32[]{:S(2)}) async-start(f32[16,1,8,83]{3,2,1,0:T(8,128)} %stack.21), calls=%async_computation.1 | async-start | bytes 131072 | tf_op jit(solution)/shard_map/all_to_all | solution.py:12
  131.3 9.2 %all-to-all-done.1 = f32[16,1,8,83]{3,2,1,0:T(8,128)S(1)} async-done(((f32[16,1,8,83]{3,2,1,0:T(8,128)}), f32[16,1,8,83]{3,2,1,0:T(8,128)S(1)}, u32[]{:S(2)}, u32[]{:S(2)}) %all-to-all-start.1) | async-done | bytes 42528 | tf_op jit(solution)/shard_map/all_to_all | solution.py:12
  140.6 1.9 %collective-permute-start.6 = (f32[1,128,83]{1,2,0:T(8,128)S(1)}, f32[1,128,83]{1,2,0:T(8,128)S(1)}, u32[]{:S(2)}, u32[]{:S(2)}) collective-permute-start(f32[1,128,83]{1,2,0:T(8,128)S(1)} %copy.198), channel_id=1, source_target_pairs={{0,16},{16,32},{32,48},{48,64},{64,80},{80,96},{96,112},{112,128},... | collective-permute-start | bytes 127496 | tf_op jit(solution)/shard_map/ppermute | solution.py:23
  142.5 8.1 %collective-permute-start.7 = (f32[1,128,83]{1,2,0:T(8,128)S(1)}, f32[1,128,83]{1,2,0:T(8,128)S(1)}, u32[]{:S(2)}, u32[]{:S(2)}) collective-permute-start(f32[1,128,83]{1,2,0:T(8,128)S(1)} %copy.198), channel_id=1, source_target_pairs={{16,0},{32,16},{48,32},{64,48},{80,64},{96,80},{112,96},{128,112},... | collective-permute-start | bytes 127496 | tf_op jit(solution)/shard_map/ppermute | solution.py:24
  150.9 0.6 collective-permute-done.7
  151.5 1.5 fusion.86
  153.1 3.2 %convolution_multiply_fusion = f32[128,8,512]{2,0,1:T(8,128)} fusion(f32[128,512]{1,0:T(8,128)S(1)} %get-tuple-element.52, f32[5,8,8,512]{3,2,1,0:T(8,128)S(1)} %bitcast.191, f32[128,83]{0,1:T(8,128)S(1)} %bitcast.228), kind=kOutput, calls=%fused_computation.5 | convolution fusion | flops 252182528 | bytes 3035136 | tf_op jit(solution)/shard_map/dot_general | solution.py:215
  156.2 1.9 %copy.207 = f32[128,8,512]{0,2,1:T(8,128)S(1)} copy(f32[128,8,512]{2,0,1:T(8,128)} %convolution_multiply_fusion) | data formatting | bytes 4194304 | tf_op jit(solution)/shard_map/mul | solution.py:222
  158.2 3.9 %fusion.128 = f32[40,4096]{1,0:T(8,128)} fusion(f32[128,4096]{0,1:T(8,128)S(1)} %bitcast.201, f32[128,83]{0,1:T(8,128)} %bitcast.229), kind=kOutput, calls=%fused_computation.187 | convolution fusion | flops 251658240 | bytes 2772992 | tf_op jit(solution)/shard_map/dot_general | solution.py:224
  162.1 3.1 %convolution_multiply_fusion.1 = f32[128,8,512]{2,0,1:T(8,128)} fusion(f32[128,512]{1,0:T(8,128)S(1)} %copy-done.5, f32[5,8,8,512]{3,2,1,0:T(8,128)S(1)} %bitcast.192, f32[128,83]{1,0:T(8,128)S(1)} %bitcast.206), kind=kOutput, calls=%fused_computation.6 | convolution fusion | flops 252182528 | bytes 3057152 | tf_op jit(solution)/shard_map/dot_general | solution.py:215
  165.2 1.9 %copy.204 = f32[128,8,512]{0,2,1:T(8,128)S(1)} copy(f32[128,8,512]{2,0,1:T(8,128)} %convolution_multiply_fusion.1) | data formatting | bytes 4194304 | tf_op jit(solution)/shard_map/mul | solution.py:222
  167.1 3.2 %fusion.112 = f32[40,4096]{1,0:T(8,128)} fusion(f32[128,4096]{0,1:T(8,128)S(1)} %bitcast.202, f32[128,83]{1,0:T(8,128)S(1)} %bitcast.207), kind=kOutput, calls=%fused_computation.170 | convolution fusion | flops 251658240 | bytes 2795008 | tf_op jit(solution)/shard_map/dot_general | solution.py:224
  170.3 3.2 %convolution_multiply_fusion.2 = f32[128,8,512]{2,0,1:T(8,128)} fusion(f32[128,512]{1,0:T(8,128)S(1)} %copy-done.3, f32[5,8,8,512]{3,2,1,0:T(8,128)S(1)} %bitcast.193, f32[128,83]{0,1:T(8,128)S(1)} %bitcast.222), kind=kOutput, calls=%fused_computation.7 | convolution fusion | flops 252182528 | bytes 3035136 | tf_op jit(solution)/shard_map/dot_general | solution.py:215
  173.5 1.9 %copy.201 = f32[128,8,512]{0,2,1:T(8,128)S(1)} copy(f32[128,8,512]{2,0,1:T(8,128)} %convolution_multiply_fusion.2) | data formatting | bytes 4194304 | tf_op jit(solution)/shard_map/mul | solution.py:222
  175.4 3.6 %fusion = f32[40,4096]{1,0:T(8,128)S(1)} fusion(f32[40,4096]{1,0:T(8,128)} %fusion.128, f32[40,4096]{1,0:T(8,128)} %fusion.112, f32[128,4096]{0,1:T(8,128)S(1)} %bitcast.198, f32[128,83]{0,1:T(8,128)S(1)} %bitcast.223), kind=kOutput, calls=%fused_computation.1 | convolution fusion | flops 251985920 | bytes 4083712 | tf_op jit(solution)/shard_map/dot_general | solution.py:224
  179.4 1.0 multiply_add_fusion.2
  (128 shorter events, 11.2 us)
Async XLA Ops:
  0.0 22.6 %copy-start = (f32[40,8,4,128]{3,2,1,0:T(4,128)S(1)}, f32[40,8,4,128]{3,2,1,0:T(4,128)}, u32[]{:S(2)}) copy-start(f32[40,8,4,128]{3,2,1,0:T(4,128)} %param.12) | copy-start | bytes 1966084
  0.0 19.1 %copy-start.10 = (s32[2,1024]{1,0:T(2,128)S(1)}, s32[2,1024]{1,0:T(2,128)}, u32[]{:S(2)}) copy-start(s32[2,1024]{1,0:T(2,128)} %param.19) | copy-start | bytes 24580
  0.0 22.0 %copy-start.19 = (f32[2,1024]{1,0:T(2,128)S(1)}, f32[2,1024]{1,0:T(2,128)}, u32[]{:S(2)}) copy-start(f32[2,1024]{1,0:T(2,128)} %param.20) | copy-start | bytes 24580
  1.8 20.8 %copy-start.16 = (s32[4,128]{1,0:T(4,128)S(1)}, s32[4,128]{1,0:T(4,128)}, u32[]{:S(2)}) copy-start(s32[4,128]{1,0:T(4,128)} %param.18) | copy-start | bytes 6148
  2.2 21.1 %collective-permute-start.1 = (f32[40,8,4,2]{0,1,3,2:T(8,128)S(1)}, f32[40,8,4,2]{0,1,3,2:T(8,128)S(1)}, u32[]{:S(2)}, u32[]{:S(2)}) collective-permute-start(f32[40,8,4,2]{0,1,3,2:T(8,128)S(1)} %copy.209), channel_id=1, source_target_pairs={{16,0},{32,16},{48,32},{64,48},{80,64},{96,80},{112,96},{128,112},... | collective-permute-start | bytes 30728 | tf_op jit(solution)/shard_map/ppermute | solution.py:24
  17.2 8.6 %collective-permute-start = (f32[40,8,4,2]{0,1,3,2:T(8,128)S(1)}, f32[40,8,4,2]{0,1,3,2:T(8,128)S(1)}, u32[]{:S(2)}, u32[]{:S(2)}) collective-permute-start(f32[40,8,4,2]{0,1,3,2:T(8,128)S(1)} %copy.208), channel_id=1, source_target_pairs={{0,16},{16,32},{32,48},{48,64},{64,80},{80,96},{96,112},{112,128},... | collective-permute-start | bytes 30728 | tf_op jit(solution)/shard_map/ppermute | solution.py:23
  21.3 0.8 copy-start.17
  27.0 9.7 %copy-start.12 = (f32[2,4,128]{2,1,0:T(4,128)S(1)}, f32[2,4,128]{2,1,0:T(4,128)}, u32[]{:S(2)}) copy-start(f32[2,4,128]{2,1,0:T(4,128)} %param.14) | copy-start | bytes 12292
  27.0 9.7 %copy-start.13 = (f32[2,4,128]{2,1,0:T(4,128)S(1)}, f32[2,4,128]{2,1,0:T(4,128)}, u32[]{:S(2)}) copy-start(f32[2,4,128]{2,1,0:T(4,128)} %param.13) | copy-start | bytes 12292
  27.1 30.1 %collective-permute-start.3 = (f32[40,8,2,132]{3,1,2,0:T(8,128)S(1)}, f32[40,8,2,132]{3,1,2,0:T(8,128)S(1)}, u32[]{:S(2)}, u32[]{:S(2)}) collective-permute-start(f32[40,8,2,132]{3,1,2,0:T(8,128)S(1)} %get-tuple-element.30), channel_id=1, source_target_pairs={{1,0},{2,1},{3,2},{4,3},{5,4},{6,5},{7,6},{8,7},{9,8},{10,9},{11,1... | collective-permute-start | bytes 1013768 | tf_op jit(solution)/shard_map/ppermute | solution.py:24
  31.1 26.4 %collective-permute-start.2 = (f32[40,8,2,132]{3,1,2,0:T(8,128)S(1)}, f32[40,8,2,132]{3,1,2,0:T(8,128)S(1)}, u32[]{:S(2)}, u32[]{:S(2)}) collective-permute-start(f32[40,8,2,132]{3,1,2,0:T(8,128)S(1)} %get-tuple-element.29), channel_id=1, source_target_pairs={{0,1},{1,2},{2,3},{3,4},{4,5},{5,6},{6,7},{7,8},{8,9},{9,10},{10,1... | collective-permute-start | bytes 1013768 | tf_op jit(solution)/shard_map/ppermute | solution.py:23
  58.0 0.7 copy-start.14
  58.0 0.9 copy-start.11
  58.6 0.7 copy-start.15
  59.3 2.2 %copy-start.20 = (f32[2,1024]{1,0:T(2,128)S(1)}, f32[2,1024]{1,0:T(2,128)}, u32[]{:S(2)}) copy-start(f32[2,1024]{1,0:T(2,128)} %param.21) | copy-start | bytes 24580
  59.3 2.5 %copy-start.7 = (f32[2,1024,40]{1,2,0:T(8,128)S(1)}, f32[2,1024,40]{1,2,0:T(8,128)}, u32[]{:S(2)}) copy-start(f32[2,1024,40]{1,2,0:T(8,128)} %param.22) | copy-start | bytes 983044
  62.8 14.9 %all-to-all-start = ((f32[16,1,8,83]{3,2,1,0:T(8,128)}), f32[16,1,8,83]{3,2,1,0:T(8,128)S(1)}, u32[]{:S(2)}, u32[]{:S(2)}) async-start(f32[16,1,8,83]{3,2,1,0:T(8,128)} %stack.20), calls=%async_computation | async-start | bytes 131072 | tf_op jit(solution)/shard_map/all_to_all | solution.py:12
  68.1 25.8 %copy-start.1 = (f32[40,4096]{1,0:T(8,128)}, f32[40,4096]{1,0:T(8,128)S(1)}, u32[]{:S(2)}) copy-start(f32[40,4096]{1,0:T(8,128)S(1)} %reshape.707) | copy-start | bytes 1966084
  77.7 13.9 %collective-permute-start.4 = (f32[1,128,83]{1,2,0:T(8,128)S(1)}, f32[1,128,83]{1,2,0:T(8,128)S(1)}, u32[]{:S(2)}, u32[]{:S(2)}) collective-permute-start(f32[1,128,83]{1,2,0:T(8,128)S(1)} %copy.184), channel_id=1, source_target_pairs={{0,16},{16,32},{32,48},{48,64},{64,80},{80,96},{96,112},{112,128},... | collective-permute-start | bytes 127496 | tf_op jit(solution)/shard_map/ppermute | solution.py:23
  84.1 8.4 %collective-permute-start.5 = (f32[1,128,83]{1,2,0:T(8,128)S(1)}, f32[1,128,83]{1,2,0:T(8,128)S(1)}, u32[]{:S(2)}, u32[]{:S(2)}) collective-permute-start(f32[1,128,83]{1,2,0:T(8,128)S(1)} %copy.184), channel_id=1, source_target_pairs={{16,0},{32,16},{48,32},{64,48},{80,64},{96,80},{112,96},{128,112},... | collective-permute-start | bytes 127496 | tf_op jit(solution)/shard_map/ppermute | solution.py:24
  92.4 1.5 copy-start.9
  99.1 3.9 %copy-start.6 = (f32[128,512]{1,0:T(8,128)S(1)}, f32[128,512]{1,0:T(8,128)}, u32[]{:S(2)}) copy-start(f32[128,512]{1,0:T(8,128)} %get-tuple-element.56) | copy-start | bytes 786436
  108.0 3.2 %copy-start.4 = (f32[128,512]{1,0:T(8,128)S(1)}, f32[128,512]{1,0:T(8,128)}, u32[]{:S(2)}) copy-start(f32[128,512]{1,0:T(8,128)} %get-tuple-element.55) | copy-start | bytes 786436
  119.9 3.2 %copy-start.22 = (pred[8]{0:T(512)(128)(4,1)S(1)}, pred[8]{0:T(512)(128)(4,1)}, u32[]{:S(2)}) copy-start(pred[8]{0:T(512)(128)(4,1)} %broadcast_compare_fusion) | copy-start | bytes 28
  121.2 2.4 %copy-start.18 = (f32[8]{0:T(128)S(1)}, f32[8]{0:T(128)}, u32[]{:S(2)}) copy-start(f32[8]{0:T(128)} %copy-done.17) | copy-start | bytes 100
  121.2 2.4 %copy-start.21 = (f32[2,1024]{1,0:T(2,128)S(1)}, f32[2,1024]{1,0:T(2,128)}, u32[]{:S(2)}) copy-start(f32[2,1024]{1,0:T(2,128)} %param.21) | copy-start | bytes 24580
  121.6 9.6 %copy-start.2 = (f32[40,4096]{1,0:T(8,128)S(1)}, f32[40,4096]{1,0:T(8,128)}, u32[]{:S(2)}) copy-start(f32[40,4096]{1,0:T(8,128)} %copy-done.1) | copy-start | bytes 1966084
  125.7 14.8 %all-to-all-start.1 = ((f32[16,1,8,83]{3,2,1,0:T(8,128)}), f32[16,1,8,83]{3,2,1,0:T(8,128)S(1)}, u32[]{:S(2)}, u32[]{:S(2)}) async-start(f32[16,1,8,83]{3,2,1,0:T(8,128)} %stack.21), calls=%async_computation.1 | async-start | bytes 131072 | tf_op jit(solution)/shard_map/all_to_all | solution.py:12
  140.6 10.3 %collective-permute-start.6 = (f32[1,128,83]{1,2,0:T(8,128)S(1)}, f32[1,128,83]{1,2,0:T(8,128)S(1)}, u32[]{:S(2)}, u32[]{:S(2)}) collective-permute-start(f32[1,128,83]{1,2,0:T(8,128)S(1)} %copy.198), channel_id=1, source_target_pairs={{0,16},{16,32},{32,48},{48,64},{64,80},{80,96},{96,112},{112,128},... | collective-permute-start | bytes 127496 | tf_op jit(solution)/shard_map/ppermute | solution.py:23
  142.5 9.0 %collective-permute-start.7 = (f32[1,128,83]{1,2,0:T(8,128)S(1)}, f32[1,128,83]{1,2,0:T(8,128)S(1)}, u32[]{:S(2)}, u32[]{:S(2)}) collective-permute-start(f32[1,128,83]{1,2,0:T(8,128)S(1)} %copy.198), channel_id=1, source_target_pairs={{16,0},{32,16},{48,32},{64,48},{80,64},{96,80},{112,96},{128,112},... | collective-permute-start | bytes 127496 | tf_op jit(solution)/shard_map/ppermute | solution.py:24
  151.5 1.5 copy-start.8
  158.2 3.9 %copy-start.5 = (f32[128,512]{1,0:T(8,128)S(1)}, f32[128,512]{1,0:T(8,128)}, u32[]{:S(2)}) copy-start(f32[128,512]{1,0:T(8,128)} %get-tuple-element.51) | copy-start | bytes 786436
  167.1 3.2 %copy-start.3 = (f32[128,512]{1,0:T(8,128)S(1)}, f32[128,512]{1,0:T(8,128)}, u32[]{:S(2)}) copy-start(f32[128,512]{1,0:T(8,128)} %get-tuple-element.50) | copy-start | bytes 786436
